TPU v7x, 32 devices: a whole 2x2x4 slice. The times are simulated.
32 devices in a mesh: group: 2 (over x), src: 16 (over z, y, core).
Axes of the slice: x: 2, y: 2, z: 4, core: 2. Of those that a mesh axis runs over, the one named last changes fastest.
Arguments:
- positions: float32 [2, 32768], P(None, ('group', 'src')), parts along dimension 1, may hold values from -0.2 to 0.2
- flux: float32 [4, 32768], P(None, ('group', 'src')), parts along dimension 1, may hold values from 0.1 to 2
- cluster: int32 [32768], P(('group', 'src')), parts along dimension 0, may hold values from 0 to 15
- jones: float32 [4, 2, 16, 1024], P(None, None, None, ('group', 'src')), parts along dimension 3, may hold values from -4 to 4
- station_uvw: float32 [3, 1024], P(None, ('group', 'src')), parts along dimension 1, may hold values from -600 to 600
- channels: int32 [8], P('group'), parts along dimension 0, may hold values from 0 to 383
- tile_map: int32 [32, 2], P('group'), parts along dimension 0, may hold values from 0 to 15, as said below
Outputs:
- visibilities: float32 [32, 4, 2, 1024], P(('group', 'src')), parts along dimension 0
There are 2 independent parts, one for each index of `group`. A program takes and returns all parts, laid end to end along the dimension named above; each array names one. Nothing has to cross between parts.
Inputs may be any that keep to these rules, and one draw needn't show every extreme that they name: `tile_map`: each row is a pair of station tiles (first, second) with first <= second; the 16 pairs are distinct.
All inputs are finite; a program needn't handle non-finite values.
Results may differ from a plain program's by a relative error of at most 0.0038.
Values sent between devices are 32-bit elements; how exact they have to be, the bound alone decides.
A program may use at most 128 MiB of HBM per device.

v0:
```python
import math

import jax
import jax.numpy as jnp
from jax import lax
from jax.sharding import PartitionSpec as P

S = 512
TS = 32


def phasors(station_gain, coords_uvw, coords, cluster_val, freq_ratio):
    directions = station_gain.shape[2]
    onehot = (cluster_val[None, :] == jnp.arange(directions, dtype=jnp.float32)[:, None]).astype(
        jnp.float32
    )
    gain_re = jnp.einsum("ckp,kn->cpn", station_gain[:, 0], onehot, precision=lax.Precision.HIGHEST)
    gain_im = jnp.einsum("ckp,kn->cpn", station_gain[:, 1], onehot, precision=lax.Precision.HIGHEST)
    l_term = coords[0]
    m_term = coords[1]
    n_term = jnp.sqrt(1.0 - l_term * l_term - m_term * m_term)
    argument = (
        coords_uvw[0][:, None] * l_term[None, :]
        + coords_uvw[1][:, None] * m_term[None, :]
        + coords_uvw[2][:, None] * (n_term - 1.0)[None, :]
    )
    phase = (2.0 * math.pi * freq_ratio)[:, None, None] * argument[None]
    cosine = jnp.cos(phase)
    sine = jnp.sin(phase)
    real_part = gain_re * cosine + gain_im * sine
    imag_part = gain_im * cosine - gain_re * sine
    return (real_part, imag_part)


def weighted_side(real_part, imag_part, fluxes, scale):
    weight = fluxes[:, None, :] * scale
    return jnp.stack([real_part * weight, imag_part * weight], 2).astype(jnp.bfloat16)


def plain_side(real_part, imag_part):
    return jnp.stack([real_part, imag_part], 2).astype(jnp.bfloat16)


def tile_products(left_sel, right_sel):
    real_sum = jnp.einsum(
        "cgirx,cgjrx->gcij", left_sel, right_sel, preferred_element_type=jnp.float32
    )
    imag_sum = jnp.einsum(
        "cgix,cgjx->gcij",
        left_sel[:, :, :, 1],
        right_sel[:, :, :, 0],
        preferred_element_type=jnp.float32,
    ) - jnp.einsum(
        "cgix,cgjx->gcij",
        left_sel[:, :, :, 0],
        right_sel[:, :, :, 1],
        preferred_element_type=jnp.float32,
    )
    return jnp.stack([real_sum, imag_sum], 2)


def clear_autos(values, pairs):
    same_tile = (pairs[:, 0] == pairs[:, 1])[:, None, None, None, None]
    diagonal = (jnp.arange(TS)[:, None] == jnp.arange(TS)[None, :])[None, None, None]
    return jnp.where(same_tile & diagonal, jnp.float32(0.0), values)


def select_stations(jones_all, uvw_all, pairs):
    chans = jones_all.shape[0]
    directions = jones_all.shape[2]
    tiles = S // TS
    count = pairs.shape[0]
    jones_tiles = jones_all.reshape(chans, 2, directions, tiles, TS)
    uvw_tiles = uvw_all.reshape(3, tiles, TS)
    first_gain = jnp.take(jones_tiles, pairs[:, 0], axis=3).reshape(
        chans, 2, directions, count * TS
    )
    second_gain = jnp.take(jones_tiles, pairs[:, 1], axis=3).reshape(
        chans, 2, directions, count * TS
    )
    first_uvw = jnp.take(uvw_tiles, pairs[:, 0], axis=1).reshape(3, count * TS)
    second_uvw = jnp.take(uvw_tiles, pairs[:, 1], axis=1).reshape(3, count * TS)
    return (first_gain, second_gain, first_uvw, second_uvw)


def add_tiles(carry, piece, stations, freq_ratio, scale, count):
    first_gain, second_gain, first_uvw, second_uvw = stations
    chans = first_gain.shape[0]
    length = piece.shape[1]
    width = math.gcd(length, 4096)

    def inner(turn, total):
        section = lax.dynamic_slice_in_dim(piece, turn * width, width, 1)
        coords = section[0:2]
        fluxes = section[2 : 2 + chans]
        kinds = section[2 + chans]
        first_re, first_im = phasors(first_gain, first_uvw, coords, kinds, freq_ratio)
        second_re, second_im = phasors(second_gain, second_uvw, coords, kinds, freq_ratio)
        left_sel = weighted_side(first_re, first_im, fluxes, scale).reshape(
            chans, count, TS, 2, width
        )
        right_sel = plain_side(second_re, second_im).reshape(chans, count, TS, 2, width)
        return total + tile_products(left_sel, right_sel)

    return lax.fori_loop(0, length // width, inner, carry)


def on_device(positions, flux, cluster, jones, station_uvw, channels, tile_map):
    freq_ratio = 1.0 + 0.002 * channels.astype(jnp.float32)
    src_dev = positions.shape[1]
    devices_src = lax.axis_size("src")
    scale = 1.0 / math.sqrt(src_dev * devices_src)
    chans = jones.shape[0]
    jones_all, uvw_all = (
        lax.all_gather(jones, "src", axis=3, tiled=True),
        lax.all_gather(station_uvw, "src", axis=1, tiled=True),
    )
    cluster_val = cluster.astype(jnp.float32)
    own_rows = tile_map.shape[0] // devices_src
    my_index = lax.axis_index("src")
    own_pairs = lax.dynamic_slice_in_dim(tile_map, my_index * own_rows, own_rows, 0)
    stations = select_stations(jones_all, uvw_all, own_pairs)
    source_rows = jnp.concatenate([positions, flux, cluster_val[None, :]], 0)
    start_total = jnp.zeros((own_rows, chans, 2, TS, TS), jnp.float32)
    total = add_tiles(
        start_total,
        lax.all_gather(source_rows, "src", axis=1, tiled=True),
        stations,
        freq_ratio,
        scale,
        own_rows,
    )
    return clear_autos(total, own_pairs).reshape(own_rows, chans, 2, TS * TS)


def solution(mesh):
    in_specs = (
        P(None, ("group", "src")),
        P(None, ("group", "src")),
        P(("group", "src")),
        P(None, None, None, ("group", "src")),
        P(None, ("group", "src")),
        P("group"),
        P("group", None),
    )
    out_specs = P(("group", "src"), None, None, None)
    return jax.shard_map(
        on_device, mesh=mesh, in_specs=in_specs, out_specs=out_specs, check_vma=False
    )
```

profile of v0, /device:TPU:0, one launch (start us, length us, event | category | flops | bytes accessed | tf_op | source)
XLA Modules:
  0.0 194.6 jit_solution(2198277265878676772)
XLA Ops:
  0.0 0.0 copy-start
  0.0 0.0 copy-start.1
  0.0 0.7 copy-done
  0.7 0.1 constant_dynamic-slice_fusion.3
  0.8 0.6 fusion.50
  5.1 1.0 copy.17
  6.1 0.0 copy-start.5
  6.1 32.3 %all_gather.10 = f32[4,2,16,512]{2,0,1,3:T(4,128)S(1)} all-gather(f32[4,2,16,32]{2,0,1,3:T(4,128)S(1)} %copy.17), channel_id=1, replica_groups=mesh['group'=2,'src'=16] {'src'}, dimensions={3}, use_global_device_ids=true | all-gather | bytes 278528 | tf_op jit(solution)/shard_map/all_gather | solution.py:115
  38.4 0.1 copy.27
  38.5 0.1 broadcast_select_fusion.1
  38.6 0.1 copy.28
  38.7 0.1 broadcast_select_fusion
  38.8 0.0 copy-done.4
  38.8 20.0 %all-gather = f32[16,32,3]{1,2,0:T(4,128)S(1)} all-gather(f32[1,32,3]{1,2,0:T(4,128)S(1)} %bitcast.161), channel_id=1, replica_groups=mesh['group'=2,'src'=16] {'src'}, dimensions={0}, use_global_device_ids=true | all-gather | bytes 6528 | tf_op jit(solution)/shard_map/all_gather | solution.py:116
  58.8 0.1 reshape.600
  58.9 0.1 reshape.480
  59.0 0.0 copy-done.3
  59.0 0.0 copy-done.2
  59.0 0.0 copy-done.1
  59.0 20.3 %all_gather.9 = f32[7,16384]{1,0:T(8,128)} all-gather(f32[7,1024]{1,0:T(8,128)S(1)} %pad_maximum_fusion), channel_id=1, replica_groups=mesh['group'=2,'src'=16] {'src'}, dimensions={1}, use_global_device_ids=true | all-gather | bytes 487424 | tf_op jit(solution)/shard_map/all_gather | solution.py:127
  79.3 0.0 copy-done.5
  79.3 113.3 %while.18 = (s32[]{:T(128)}, f32[1,4,2,32,32]{4,3,1,2,0:T(8,128)S(1)}, f32[7,16384]{1,0:T(8,128)}, f32[4,2,16,32]{3,2,0,1:T(8,128)S(1)}, f32[4]{0:T(128)S(1)}, /...) while((s32[]{:T(128)}, ...), condition=%wide.region_1.0_spmd.clone, body=%wide.region_0.3_spmd.clone.sunk | while | flops 551092224 | bytes 27986972 | solution.py:105
  79.3 1.2 sqrt_add_fusion.2
  80.6 0.2 multiply_add_fusion.4
  80.8 1.0 convolution_bitcast_fusion.7
  81.8 2.4 %convolution_bitcast_fusion.8 = f32[4,32,4096]{2,1,0:T(8,128)} fusion(f32[4096]{0:T(1024)S(1)} %bitcast.150, f32[4,2,16,32]{3,2,0,1:T(8,128)S(1)} %get-tuple-element.430), kind=kOutput, calls=%fused_computation.3.clone.1 | convolution fusion | flops 100728832 | bytes 2146304 | tf_op jit(solution)/shard_map/while/body/eval_jaxpr/ckp,kn->cpn/dot_general | solution.py:17
  84.2 2.3 %convolution_bitcast_fusion.9 = f32[4,32,4096]{2,1,0:T(8,128)} fusion(f32[4096]{0:T(1024)S(1)} %bitcast.151, f32[4,2,16,32]{3,2,0,1:T(8,128)S(1)} %get-tuple-element.430), kind=kOutput, calls=%fused_computation.2.clone.1 | convolution fusion | flops 100728832 | bytes 2146304 | tf_op jit(solution)/shard_map/while/body/eval_jaxpr/ckp,kn->cpn/dot_general | solution.py:18
  86.5 1.0 dynamic-slice_multiply_fusion.2
  87.6 18.3 %fusion.84 = (bf16[4,32,4096]{2,1,0:T(8,128)(2,1)S(1)}, bf16[4,32,4096]{2,1,0:T(8,128)(2,1)S(1)}, bf16[4,32,4096]{2,1,0:T(8,128)(2,1)S(1)}, bf16[4,32,4096]{2,1,0:T(8,128)(2,1)S(1)}) fusion(f32[4,32,4096]{2,1,0:T(8,128)S(1)} %convolution_bitcast_fusion.7, f32[32,4096]{1,0:T(8,128)S(1)} %get-tuple-element.391, f32[4]{0:T(128)S(1)} %broadcast_multiply_fusion.2, ...), kind=kOutput, calls=%fused_computation.19.clone.1 | convolution fusion | flops 111214592 | bytes 11649536 | tf_op jit(solution)/shard_map/while/body/eval_jaxpr/ckp,kn->cpn/dot_general | solution.py:17
  105.9 0.8 fusion.87
  106.7 0.4 fusion.85
  107.1 0.4 fusion.86
  107.6 1.2 sqrt_add_fusion.2
  108.9 0.2 multiply_add_fusion.4
  109.1 1.0 convolution_bitcast_fusion.7
  110.1 2.4 %convolution_bitcast_fusion.8 = f32[4,32,4096]{2,1,0:T(8,128)} fusion(f32[4096]{0:T(1024)S(1)} %bitcast.150, f32[4,2,16,32]{3,2,0,1:T(8,128)S(1)} %get-tuple-element.430), kind=kOutput, calls=%fused_computation.3.clone.1 | convolution fusion | flops 100728832 | bytes 2146304 | tf_op jit(solution)/shard_map/while/body/eval_jaxpr/ckp,kn->cpn/dot_general | solution.py:17
  112.5 2.3 %convolution_bitcast_fusion.9 = f32[4,32,4096]{2,1,0:T(8,128)} fusion(f32[4096]{0:T(1024)S(1)} %bitcast.151, f32[4,2,16,32]{3,2,0,1:T(8,128)S(1)} %get-tuple-element.430), kind=kOutput, calls=%fused_computation.2.clone.1 | convolution fusion | flops 100728832 | bytes 2146304 | tf_op jit(solution)/shard_map/while/body/eval_jaxpr/ckp,kn->cpn/dot_general | solution.py:18
  114.9 1.0 dynamic-slice_multiply_fusion.2
  115.9 18.3 %fusion.84 = (bf16[4,32,4096]{2,1,0:T(8,128)(2,1)S(1)}, bf16[4,32,4096]{2,1,0:T(8,128)(2,1)S(1)}, bf16[4,32,4096]{2,1,0:T(8,128)(2,1)S(1)}, bf16[4,32,4096]{2,1,0:T(8,128)(2,1)S(1)}) fusion(f32[4,32,4096]{2,1,0:T(8,128)S(1)} %convolution_bitcast_fusion.7, f32[32,4096]{1,0:T(8,128)S(1)} %get-tuple-element.391, f32[4]{0:T(128)S(1)} %broadcast_multiply_fusion.2, ...), kind=kOutput, calls=%fused_computation.19.clone.1 | convolution fusion | flops 111214592 | bytes 11649536 | tf_op jit(solution)/shard_map/while/body/eval_jaxpr/ckp,kn->cpn/dot_general | solution.py:17
  134.2 0.9 fusion.87
  135.1 0.4 fusion.85
  135.5 0.4 fusion.86
  136.0 1.2 sqrt_add_fusion.2
  137.2 0.2 multiply_add_fusion.4
  137.4 1.0 convolution_bitcast_fusion.7
  138.5 2.4 %convolution_bitcast_fusion.8 = f32[4,32,4096]{2,1,0:T(8,128)} fusion(f32[4096]{0:T(1024)S(1)} %bitcast.150, f32[4,2,16,32]{3,2,0,1:T(8,128)S(1)} %get-tuple-element.430), kind=kOutput, calls=%fused_computation.3.clone.1 | convolution fusion | flops 100728832 | bytes 2146304 | tf_op jit(solution)/shard_map/while/body/eval_jaxpr/ckp,kn->cpn/dot_general | solution.py:17
  140.8 2.3 %convolution_bitcast_fusion.9 = f32[4,32,4096]{2,1,0:T(8,128)} fusion(f32[4096]{0:T(1024)S(1)} %bitcast.151, f32[4,2,16,32]{3,2,0,1:T(8,128)S(1)} %get-tuple-element.430), kind=kOutput, calls=%fused_computation.2.clone.1 | convolution fusion | flops 100728832 | bytes 2146304 | tf_op jit(solution)/shard_map/while/body/eval_jaxpr/ckp,kn->cpn/dot_general | solution.py:18
  143.2 1.0 dynamic-slice_multiply_fusion.2
  144.2 18.3 %fusion.84 = (bf16[4,32,4096]{2,1,0:T(8,128)(2,1)S(1)}, bf16[4,32,4096]{2,1,0:T(8,128)(2,1)S(1)}, bf16[4,32,4096]{2,1,0:T(8,128)(2,1)S(1)}, bf16[4,32,4096]{2,1,0:T(8,128)(2,1)S(1)}) fusion(f32[4,32,4096]{2,1,0:T(8,128)S(1)} %convolution_bitcast_fusion.7, f32[32,4096]{1,0:T(8,128)S(1)} %get-tuple-element.391, f32[4]{0:T(128)S(1)} %broadcast_multiply_fusion.2, ...), kind=kOutput, calls=%fused_computation.19.clone.1 | convolution fusion | flops 111214592 | bytes 11649536 | tf_op jit(solution)/shard_map/while/body/eval_jaxpr/ckp,kn->cpn/dot_general | solution.py:17
  162.5 0.9 fusion.87
  163.4 0.4 fusion.85
  163.8 0.4 fusion.86
  164.3 1.2 sqrt_add_fusion.2
  165.5 0.2 multiply_add_fusion.4
  165.8 1.0 convolution_bitcast_fusion.7
  166.8 2.4 %convolution_bitcast_fusion.8 = f32[4,32,4096]{2,1,0:T(8,128)} fusion(f32[4096]{0:T(1024)S(1)} %bitcast.150, f32[4,2,16,32]{3,2,0,1:T(8,128)S(1)} %get-tuple-element.430), kind=kOutput, calls=%fused_computation.3.clone.1 | convolution fusion | flops 100728832 | bytes 2146304 | tf_op jit(solution)/shard_map/while/body/eval_jaxpr/ckp,kn->cpn/dot_general | solution.py:17
  169.2 2.3 %convolution_bitcast_fusion.9 = f32[4,32,4096]{2,1,0:T(8,128)} fusion(f32[4096]{0:T(1024)S(1)} %bitcast.151, f32[4,2,16,32]{3,2,0,1:T(8,128)S(1)} %get-tuple-element.430), kind=kOutput, calls=%fused_computation.2.clone.1 | convolution fusion | flops 100728832 | bytes 2146304 | tf_op jit(solution)/shard_map/while/body/eval_jaxpr/ckp,kn->cpn/dot_general | solution.py:18
  171.5 1.0 dynamic-slice_multiply_fusion.2
  172.5 18.3 %fusion.84 = (bf16[4,32,4096]{2,1,0:T(8,128)(2,1)S(1)}, bf16[4,32,4096]{2,1,0:T(8,128)(2,1)S(1)}, bf16[4,32,4096]{2,1,0:T(8,128)(2,1)S(1)}, bf16[4,32,4096]{2,1,0:T(8,128)(2,1)S(1)}) fusion(f32[4,32,4096]{2,1,0:T(8,128)S(1)} %convolution_bitcast_fusion.7, f32[32,4096]{1,0:T(8,128)S(1)} %get-tuple-element.391, f32[4]{0:T(128)S(1)} %broadcast_multiply_fusion.2, ...), kind=kOutput, calls=%fused_computation.19.clone.1 | convolution fusion | flops 111214592 | bytes 11649536 | tf_op jit(solution)/shard_map/while/body/eval_jaxpr/ckp,kn->cpn/dot_general | solution.py:17
  190.8 0.8 fusion.87
  191.7 0.4 fusion.85
  192.1 0.4 fusion.86
  193.9 0.1 reshape.607
  194.0 0.6 copy.24
  (27 shorter events, 0.3 us)
Async XLA Ops:
  0.0 0.7 copy-start
  0.0 38.8 %copy-start.4 = (f32[3,32]{1,0:T(4,128)S(1)}, f32[3,32]{1,0:T(4,128)}, u32[]{:S(2)}) copy-start(f32[3,32]{1,0:T(4,128)} %param.17) | copy-start | bytes 1156
  0.0 59.0 %copy-start.3 = (s32[1024]{0:T(1024)S(1)}, s32[1024]{0:T(1024)}, u32[]{:S(2)}) copy-start(s32[1024]{0:T(1024)} %param.15) | copy-start | bytes 12292
  0.0 59.0 %copy-start.2 = (f32[2,1024]{1,0:T(2,128)S(1)}, f32[2,1024]{1,0:T(2,128)}, u32[]{:S(2)}) copy-start(f32[2,1024]{1,0:T(2,128)} %param.13) | copy-start | bytes 24580
  0.0 59.0 %copy-start.1 = (f32[4,1024]{1,0:T(4,128)S(1)}, f32[4,1024]{1,0:T(4,128)}, u32[]{:S(2)}) copy-start(f32[4,1024]{1,0:T(4,128)} %param.14) | copy-start | bytes 49156
  6.1 73.3 %copy-start.5 = (s32[4]{0:T(128)S(1)}, s32[4]{0:T(128)}, u32[]{:S(2)}) copy-start(s32[4]{0:T(128)} %param.18) | copy-start | bytes 52
where the time goes:
time: 195 us
  matrix products  103 us (53%)
  blocking collectives  72.6 us (37%)
  other arithmetic  10.1 us (5%)
  between operations  5.16 us (3%)
  local copies, waits for them, and re-layouts  3.49 us (2%)
    dot_general x8, matrix products, phasors(): jnp.einsum('ckp,kn->cpn', station_gain[:, 0], onehot, precision=lax.Preci...  82.7 us
    all_gather x1, blocking collectives, on_device(): lax.all_gather(jones, 'src', axis=3, tiled=True)  32.3 us
    all_gather x1, blocking collectives, on_device(): lax.all_gather(source_rows, 'src', axis=1, tiled=True)  20.3 us
    all_gather x1, blocking collectives, on_device(): lax.all_gather(station_uvw, 'src', axis=1, tiled=True)  20 us
    dot_general x8, matrix products, phasors(): jnp.einsum('ckp,kn->cpn', station_gain[:, 1], onehot, precision=lax.Preci...  13.5 us
    sub x4, other arithmetic, phasors(): n_term - 1.0  4.79 us
    mul x4, other arithmetic, weighted_side(): weight = fluxes[:, None, :] * scale  4 us

commit v1 on v0

v1 whole, which is shorter than its diff:
```python
import functools
import math

import jax
import jax.numpy as jnp
from jax import lax
from jax.experimental import pallas as pl
from jax.experimental.pallas import tpu as pltpu
from jax.sharding import PartitionSpec as P

MESH = pl.DeviceIdType.MESH
TS = 32
GROUP = 64
HALF = 32
CHUNK = 256
MAGIC = 12582912.0
COS = (
    0.9999992251396179,
    -19.738977432250977,
    64.9285888671875,
    -85.27084350585938,
    58.78694152832031,
    -21.0654296875,
)
SIN = (
    6.283185005187988,
    -41.34158706665039,
    81.59991455078125,
    -76.61414337158203,
    41.341365814208984,
    -12.468818664550781,
)


def horner(coefs, y):
    total = jnp.float32(coefs[-1])
    for coef in coefs[-2::-1]:
        total = total * y + jnp.float32(coef)
    return total


def three_parts(value):
    first = value.astype(jnp.bfloat16).astype(jnp.float32)
    rest = value - first
    second = rest.astype(jnp.bfloat16).astype(jnp.float32)
    return first, second, rest - second


def kernel(
    devices,
    chans,
    dirs,
    scale,
    tile_ref,
    station_ref,
    source_ref,
    out_ref,
    stations,
    sources,
    table,
    onehots,
    acc,
    st_send,
    st_recv,
    st_fwd_send,
    st_fwd_recv,
    so_send,
    so_recv,
    so_fwd_send,
    so_fwd_recv,
    own_sem,
):
    chips = devices // 2
    me = lax.axis_index("src")
    chip = me // 2
    core = lax.rem(me, 2)
    partner = chip * 2 + 1 - core
    rows = stations.shape[1]
    per_dev = rows * 2 // chans
    width = sources.shape[2]

    own = [
        pltpu.make_async_copy(station_ref, stations.at[me], own_sem.at[0]),
        pltpu.make_async_copy(source_ref, sources.at[me], own_sem.at[1]),
    ]
    for copy in own:
        copy.start()

    barrier = pltpu.get_barrier_semaphore()

    def greet(k, carry):
        there = lax.rem(chip + k, chips) * 2 + core
        pl.semaphore_signal(barrier, inc=1, device_id={"src": there}, device_id_type=MESH)
        return carry

    pl.semaphore_signal(barrier, inc=1, device_id={"src": partner}, device_id_type=MESH)
    lax.fori_loop(1, chips, greet, 0)
    pl.semaphore_wait(barrier, chips)

    def direct(mine, slots, send, recv, k):
        there = lax.rem(chip + k, chips) * 2 + core
        return pltpu.make_async_remote_copy(
            src_ref=mine,
            dst_ref=slots.at[me],
            send_sem=send.at[k],
            recv_sem=recv.at[k],
            device_id={"src": there},
            device_id_type=MESH,
        )

    def arrival(mine, slots, send, recv, k):
        came = lax.rem(chip - k + chips, chips) * 2 + core
        return pltpu.make_async_remote_copy(
            src_ref=mine,
            dst_ref=slots.at[came],
            send_sem=send.at[k],
            recv_sem=recv.at[k],
            device_id={"src": partner},
            device_id_type=MESH,
        )

    def forward(slots, send, recv, k):
        came = lax.rem(chip - k + chips, chips) * 2 + core
        return pltpu.make_async_remote_copy(
            src_ref=slots.at[came],
            dst_ref=slots.at[came],
            send_sem=send.at[k],
            recv_sem=recv.at[k],
            device_id={"src": partner},
            device_id_type=MESH,
        )

    def forwarded(slots, send, recv, k):
        came = lax.rem(chip - k + chips, chips) * 2 + 1 - core
        return pltpu.make_async_remote_copy(
            src_ref=slots.at[came],
            dst_ref=slots.at[came],
            send_sem=send.at[k],
            recv_sem=recv.at[k],
            device_id={"src": partner},
            device_id_type=MESH,
        )

    for copy in own:
        copy.wait()
    forward(stations, st_fwd_send, st_fwd_recv, 0).start()

    def send_stations(k, carry):
        direct(station_ref, stations, st_send, st_recv, k).start()
        return carry

    lax.fori_loop(1, chips, send_stations, 0)
    forward(sources, so_fwd_send, so_fwd_recv, 0).start()

    def send_sources(k, carry):
        direct(source_ref, sources, so_send, so_recv, k).start()
        return carry

    lax.fori_loop(1, chips, send_sources, 0)

    onehots[3 * GROUP :, :] = jnp.zeros((GROUP, width), jnp.bfloat16)
    for part in range(3):
        onehots[part * GROUP + HALF + dirs : (part + 1) * GROUP, :] = jnp.zeros(
            (GROUP - HALF - dirs, width), jnp.bfloat16
        )
    acc[...] = jnp.zeros_like(acc)

    def relay_stations(k, carry):
        arrival(station_ref, stations, st_send, st_recv, k).wait_recv()
        forward(stations, st_fwd_send, st_fwd_recv, k).start()
        return carry

    lax.fori_loop(1, chips, relay_stations, 0)

    def take_stations(k, carry):
        forwarded(stations, st_fwd_send, st_fwd_recv, k).wait_recv()
        return carry

    lax.fori_loop(0, chips, take_stations, 0)

    per_tile = TS // per_dev
    lane = lax.broadcasted_iota(jnp.int32, (TS, 128), 1)
    is_phase = lax.rem(lane, GROUP) < HALF
    low = lane < GROUP
    half_rows = chans * TS
    tiles = [tile_ref[me, 0], tile_ref[me, 1]]
    for side in range(2):
        held = [stations[tiles[side] * per_tile + d] for d in range(per_tile)]
        for c in range(chans):
            begin = c // 2 * per_dev
            value = jnp.concatenate([part[begin : begin + per_dev] for part in held], 0)
            if c % 2:
                value = pltpu.roll(value, GROUP, 1)
            value = jnp.where(low, value, 0.0)
            first, second, third = three_parts(value)
            pieces = [first + pltpu.roll(second, GROUP, 1), third]
            at = side * half_rows + c * TS
            for index, piece in enumerate(pieces):
                cols = slice(index * 128, index * 128 + 128)
                table[at : at + TS, cols] = jnp.where(is_phase, piece, 0.0).astype(jnp.bfloat16)
                below = 2 * half_rows + at
                table[below : below + TS, cols] = jnp.where(is_phase, 0.0, piece).astype(
                    jnp.bfloat16
                )

    def block(step, carry):
        k = step // 2
        odd = lax.rem(step, 2)

        @pl.when(jnp.logical_and(odd == 0, k > 0))
        def _():
            arrival(source_ref, sources, so_send, so_recv, k).wait_recv()
            forward(sources, so_fwd_send, so_fwd_recv, k).start()

        @pl.when(odd == 1)
        def _():
            forwarded(sources, so_fwd_send, so_fwd_recv, k).wait_recv()

        flip = core + odd - 2 * core * odd
        came = lax.rem(chip - k + chips, chips) * 2 + flip
        l_term = sources[came, 0:1, :]
        m_term = sources[came, 1:2, :]
        kinds = sources[came, 2 + chans : 3 + chans, :]
        n_less = jnp.sqrt(1.0 - l_term * l_term - m_term * m_term) - 1.0
        sub = lax.broadcasted_iota(jnp.int32, (16, width), 0)
        coords = jnp.zeros((16, width), jnp.float32)
        for axis, term in enumerate((l_term, m_term, n_less)):
            for index, part in enumerate(three_parts(term)):
                coords = jnp.where(sub == index * 3 + axis, part, coords)
        kind_rows = lax.broadcasted_iota(jnp.int32, (dirs, width), 0).astype(jnp.float32)
        onehot = jnp.where(kind_rows == kinds, 1.0, 0.0).astype(jnp.bfloat16)
        coords = coords.astype(jnp.bfloat16)
        for part in range(3):
            base = part * GROUP
            onehots[base : base + dirs, :] = onehot
            onehots[base + dirs : base + dirs + 16, :] = coords
            onehots[base + HALF : base + HALF + dirs, :] = onehot

        total = acc[...]
        for chunk in range(width // CHUNK):
            cols = slice(chunk * CHUNK, chunk * CHUNK + CHUNK)
            weights = onehots[:, cols]
            sides = []
            for side in range(2):
                real, imag = [], []
                for c in range(chans):
                    at = side * half_rows + c * TS
                    below = 2 * half_rows + at
                    turns = jnp.dot(
                        table[at : at + TS, :], weights, preferred_element_type=jnp.float32
                    )
                    size = jnp.dot(
                        table[below : below + TS, :], weights, preferred_element_type=jnp.float32
                    )
                    if side == 0:
                        size = size * (sources[came, 2 + c : 3 + c, cols] * scale)
                    turns = turns - ((turns + MAGIC) - MAGIC)
                    square = turns * turns
                    real.append((size * horner(COS, square)).astype(jnp.bfloat16))
                    imag.append((size * (turns * horner(SIN, square))).astype(jnp.bfloat16))
                sides.append(jnp.concatenate(real + imag, 0))
            total = total + lax.dot_general(
                sides[0],
                sides[1],
                (((1,), (1,)), ((), ())),
                preferred_element_type=jnp.float32,
            )
        acc[...] = total
        return carry

    lax.fori_loop(0, 2 * chips, block, 0)

    same = tiles[0] == tiles[1]
    diagonal = lax.broadcasted_iota(jnp.int32, (TS, TS), 0) == lax.broadcasted_iota(
        jnp.int32, (TS, TS), 1
    )
    clear = jnp.logical_and(diagonal, same)
    for c in range(chans):
        top = slice(c * TS, c * TS + TS)
        low_rows = slice(half_rows + c * TS, half_rows + c * TS + TS)
        real_rows = acc[top, :]
        imag_rows = acc[low_rows, :]
        real = real_rows[:, top] + imag_rows[:, low_rows]
        imag = real_rows[:, low_rows] - imag_rows[:, top]
        for part, value in enumerate((real, imag)):
            value = jnp.where(clear, 0.0, value)
            for i in range(TS):
                out_ref[0, c, part : part + 1, i * TS : i * TS + TS] = value[i : i + 1, :]

    def finish(k, carry):
        direct(station_ref, stations, st_send, st_recv, k).wait_send()
        direct(source_ref, sources, so_send, so_recv, k).wait_send()
        return carry

    lax.fori_loop(1, chips, finish, 0)

    def finish_forward(k, carry):
        forward(stations, st_fwd_send, st_fwd_recv, k).wait_send()
        forward(sources, so_fwd_send, so_fwd_recv, k).wait_send()
        return carry

    lax.fori_loop(0, chips, finish_forward, 0)


def on_device(positions, flux, cluster, jones, station_uvw, channels, tile_map):
    freq_ratio = 1.0 + 0.002 * channels.astype(jnp.float32)
    width = positions.shape[1]
    devices = lax.axis_size("src")
    scale = 1.0 / math.sqrt(width * devices)
    chans, _, dirs, per_dev = jones.shape

    large = jnp.maximum(jnp.abs(jones[:, 0]), jnp.abs(jones[:, 1]))
    small = jnp.minimum(jnp.abs(jones[:, 0]), jnp.abs(jones[:, 1]))
    ratio = small / jnp.where(large > 0.0, large, 1.0)
    size = large * jnp.sqrt(1.0 + ratio * ratio)
    angle = jnp.arctan2(jones[:, 1], jones[:, 0]) * (-0.5 / math.pi)
    coords = freq_ratio[:, None, None] * station_uvw[None]
    features = jnp.concatenate(
        [
            angle,
            coords,
            coords,
            coords,
            jnp.zeros((chans, HALF - dirs - 9, per_dev), jnp.float32),
            size,
            jnp.zeros((chans, GROUP - HALF - dirs, per_dev), jnp.float32),
        ],
        1,
    )
    own_stations = (
        features.reshape(chans // 2, 2 * GROUP, per_dev)
        .transpose(0, 2, 1)
        .reshape(chans // 2 * per_dev, 2 * GROUP)
    )
    own_sources = jnp.concatenate(
        [
            positions,
            flux,
            cluster.astype(jnp.float32)[None],
            jnp.zeros((8 - 3 - chans, width), jnp.float32),
        ],
        0,
    )
    wide = 2 * chans * TS
    chips = devices // 2
    vmem = pl.BlockSpec(memory_space=pltpu.VMEM)
    return pl.pallas_call(
        functools.partial(kernel, devices, chans, dirs, scale),
        out_shape=jax.ShapeDtypeStruct((1, chans, 2, TS * TS), jnp.float32),
        in_specs=[pl.BlockSpec(memory_space=pltpu.SMEM), vmem, vmem],
        out_specs=vmem,
        scratch_shapes=[
            pltpu.VMEM((devices,) + own_stations.shape, jnp.float32),
            pltpu.VMEM((devices,) + own_sources.shape, jnp.float32),
            pltpu.VMEM((2 * wide, 4 * GROUP), jnp.bfloat16),
            pltpu.VMEM((4 * GROUP, width), jnp.bfloat16),
            pltpu.VMEM((wide, wide), jnp.float32),
        ]
        + [pltpu.SemaphoreType.DMA((chips,))] * 8
        + [pltpu.SemaphoreType.DMA((2,))],
        compiler_params=pltpu.CompilerParams(collective_id=0, has_side_effects=True),
    )(tile_map, own_stations, own_sources)


def solution(mesh):
    in_specs = (
        P(None, ("group", "src")),
        P(None, ("group", "src")),
        P(("group", "src")),
        P(None, None, None, ("group", "src")),
        P(None, ("group", "src")),
        P("group"),
        P("group", None),
    )
    out_specs = P(("group", "src"), None, None, None)
    return jax.shard_map(
        on_device, mesh=mesh, in_specs=in_specs, out_specs=out_specs, check_vma=False
    )
```

time: 195 us -> 61.3 us (0.31)
  the two profiles are of different devices: /device:TPU:0 before, /device:TPU:31 now
where the time goes in v1:
time: 61.3 us; the launch traced here: 60.9 us
  Pallas kernels  55 us (90%)
  local copies, waits for them, and re-layouts  4.19 us (7%)
  other arithmetic  1.69 us (3%)
    pallas_call x1, Pallas kernels, on_device(): pl.pallas_call(functools.partial(kernel, devices, chans, dirs, scale), ou...  55 us
    unnamed x16, local copies, waits for them, and re-layouts  3.29 us

profile of v1, /device:TPU:31, one launch (start us, length us, event | category | flops | bytes accessed | tf_op | source)
XLA Modules:
  0.0 60.9 jit_solution(6984095771036642409)
XLA Ops:
  0.0 0.0 copy-start
  0.0 0.9 %fusion.4 = f32[4,16,32]{2,1,0:T(8,128)S(1)} fusion(f32[4,2,16,32]{3,2,1,0:T(8,128)} %param.10), kind=kLoop, calls=%fused_computation.5 | loop fusion | flops 20480 | bytes 24576 | tf_op jit(solution)/shard_map/mul | solution.py:315
  0.9 0.0 copy-done
  0.9 0.0 copy-start.6
  0.9 0.0 copy-start.4
  0.9 0.1 fusion.6
  1.0 0.6 copy-done.6
  1.5 0.0 copy-done.4
  1.6 0.1 broadcast_multiply_fusion
  1.7 0.1 concatenate.6
  1.8 0.0 copy-start.3
  1.8 0.0 copy-start.1
  1.8 0.7 %copy.12 = f32[2,128,32]{1,2,0:T(8,128)} copy(f32[2,128,32]{2,1,0:T(8,128)S(1)} %bitcast.31) | data formatting | bytes 65536 | tf_op jit(solution)/shard_map/reshape | solution.py:331
  2.5 0.0 copy-start.2
  2.5 0.0 copy-done.3
  2.5 0.1 pad.3.clone
  2.6 0.0 copy-done.1
  2.6 0.6 %copy-done.2 = f32[2,1024]{1,0:T(2,128)S(1)} copy-done((f32[2,1024]{1,0:T(2,128)S(1)}, f32[2,1024]{1,0:T(2,128)}, u32[]{:S(2)}) %copy-start.2) | copy-done | bytes 8216
  3.2 0.0 copy-start.5
  3.2 0.7 %maximum_maximum_fusion.source_ref = f32[8,1024]{1,0:T(8,128)} fusion(f32[1,1024]{1,0:T(1,128)S(1)} %bitcast.33, f32[4,1024]{1,0:T(4,128)S(1)} %copy-done.1, f32[2,1024]{1,0:T(2,128)S(1)} %copy-done.2, f32[8]{0:T(128)S(1)} %pad.3.clone), kind=kLoop, calls=%fused_computation.6 | loop fusion | flops 24576 | bytes 61472 | tf_op jit(solution)/shard_map/concatenate | solution.py:335
  3.9 0.0 copy-done.5
  3.9 0.7 %copy.13.tile_ref = s32[16,2]{1,0:T(8,128)} copy(s32[16,2]{0,1:T(2,128)S(1)} %copy-done.5) | data formatting | bytes 256 | tf_op args[6]
  4.6 55.0 %shard_map.73 = f32[1,4,2,1024]{3,2,1,0:T(2,128)} custom-call(s32[16,2]{1,0:T(8,128)} %copy.13.tile_ref, f32[64,128]{1,0:T(8,128)} %bitcast.32, f32[8,1024]{1,0:T(8,128)} %maximum_maximum_fusion.source_ref), custom_call_target="tpu_custom_call" | custom-call | tf_op jit(solution)/shard_map/pallas_call | solution.py:347
  59.6 1.4 %copy.16 = f32[1,4,2,1024]{3,2,1,0:T(2,128)} copy(f32[1,4,2,1024]{3,2,1,0:T(2,128)} %shard_map.73) | data formatting | bytes 65536
  (4 shorter events, 0.0 us)
Async XLA Ops:
  0.0 0.9 %copy-start = (f32[4,2,16,32]{3,2,1,0:T(8,128)S(1)}, f32[4,2,16,32]{3,2,1,0:T(8,128)}, u32[]{:S(2)}) copy-start(f32[4,2,16,32]{3,2,1,0:T(8,128)} %param.10) | copy-start | bytes 49156
  0.9 0.7 %copy-start.6 = (s32[4]{0:T(128)S(1)}, s32[4]{0:T(128)}, u32[]{:S(2)}) copy-start(s32[4]{0:T(128)} %param.12) | copy-start | bytes 52
  0.9 0.7 %copy-start.4 = (f32[3,32]{1,0:T(4,128)S(1)}, f32[3,32]{1,0:T(4,128)}, u32[]{:S(2)}) copy-start(f32[3,32]{1,0:T(4,128)} %param.11) | copy-start | bytes 1156
  1.8 0.7 %copy-start.3 = (s32[1024]{0:T(1024)S(1)}, s32[1024]{0:T(1024)}, u32[]{:S(2)}) copy-start(s32[1024]{0:T(1024)} %param.9) | copy-start | bytes 12292
  1.8 0.8 %copy-start.1 = (f32[4,1024]{1,0:T(4,128)S(1)}, f32[4,1024]{1,0:T(4,128)}, u32[]{:S(2)}) copy-start(f32[4,1024]{1,0:T(4,128)} %param.8) | copy-start | bytes 49156
  2.5 0.7 %copy-start.2 = (f32[2,1024]{1,0:T(2,128)S(1)}, f32[2,1024]{1,0:T(2,128)}, u32[]{:S(2)}) copy-start(f32[2,1024]{1,0:T(2,128)} %param.7) | copy-start | bytes 24580
  3.2 0.7 %copy-start.5 = (s32[16,2]{0,1:T(2,128)S(1)}, s32[16,2]{0,1:T(2,128)}, u32[]{:S(2)}) copy-start(s32[16,2]{0,1:T(2,128)} %param.13) | copy-start | bytes 388

commit v2 on v1

--- a/solution.py
+++ b/solution.py
@@ -13,23 +13,8 @@
 GROUP = 64
 HALF = 32
 CHUNK = 256
-MAGIC = 12582912.0
-COS = (
-    0.9999992251396179,
-    -19.738977432250977,
-    64.9285888671875,
-    -85.27084350585938,
-    58.78694152832031,
-    -21.0654296875,
-)
-SIN = (
-    6.283185005187988,
-    -41.34158706665039,
-    81.59991455078125,
-    -76.61414337158203,
-    41.341365814208984,
-    -12.468818664550781,
-)
+SINE = (3.1415820121765137, -5.167142868041992, 2.5418992042541504, -0.5546366572380066)
+ONE = 1.0 + 6e-7
 
 
 def horner(coefs, y):
@@ -59,6 +44,7 @@
     sources,
     table,
     onehots,
+    sides,
     acc,
     st_send,
     st_recv,
@@ -194,11 +180,11 @@
             value = jnp.where(low, value, 0.0)
             first, second, third = three_parts(value)
             pieces = [first + pltpu.roll(second, GROUP, 1), third]
-            at = side * half_rows + c * TS
+            at = (side * chans + c) * 2 * TS
             for index, piece in enumerate(pieces):
                 cols = slice(index * 128, index * 128 + 128)
                 table[at : at + TS, cols] = jnp.where(is_phase, piece, 0.0).astype(jnp.bfloat16)
-                below = 2 * half_rows + at
+                below = at + TS
                 table[below : below + TS, cols] = jnp.where(is_phase, 0.0, piece).astype(
                     jnp.bfloat16
                 )
@@ -236,36 +222,35 @@
             onehots[base + dirs : base + dirs + 16, :] = coords
             onehots[base + HALF : base + HALF + dirs, :] = onehot
 
-        total = acc[...]
         for chunk in range(width // CHUNK):
             cols = slice(chunk * CHUNK, chunk * CHUNK + CHUNK)
             weights = onehots[:, cols]
-            sides = []
+            found = jnp.dot(table[...], weights, preferred_element_type=jnp.float32)
             for side in range(2):
-                real, imag = [], []
                 for c in range(chans):
-                    at = side * half_rows + c * TS
-                    below = 2 * half_rows + at
-                    turns = jnp.dot(
-                        table[at : at + TS, :], weights, preferred_element_type=jnp.float32
+                    at = (side * chans + c) * 2 * TS
+                    turns = found[at : at + TS]
+                    double = found[at + TS : at + 2 * TS]
+                    if side == 0:
+                        double = double * (sources[came, 2 + c : 3 + c, cols] * scale)
+                    turns = turns - jnp.round(turns)
+                    sine = turns * horner(SINE, turns * turns)
+                    square = sine * sine
+                    rest = ONE - square
+                    cosine = rest * lax.rsqrt(rest)
+                    real = double * (0.5 - square)
+                    imag = (double * sine) * cosine
+                    top = c * TS
+                    sides[side, top : top + TS, cols] = real.astype(jnp.bfloat16)
+                    sides[side, half_rows + top : half_rows + top + TS, cols] = imag.astype(
+                        jnp.bfloat16
                     )
-                    size = jnp.dot(
-                        table[below : below + TS, :], weights, preferred_element_type=jnp.float32
-                    )
-                    if side == 0:
-                        size = size * (sources[came, 2 + c : 3 + c, cols] * scale)
-                    turns = turns - ((turns + MAGIC) - MAGIC)
-                    square = turns * turns
-                    real.append((size * horner(COS, square)).astype(jnp.bfloat16))
-                    imag.append((size * (turns * horner(SIN, square))).astype(jnp.bfloat16))
-                sides.append(jnp.concatenate(real + imag, 0))
-            total = total + lax.dot_general(
-                sides[0],
-                sides[1],
-                (((1,), (1,)), ((), ())),
-                preferred_element_type=jnp.float32,
-            )
-        acc[...] = total
+        acc[...] += lax.dot_general(
+            sides[0],
+            sides[1],
+            (((1,), (1,)), ((), ())),
+            preferred_element_type=jnp.float32,
+        )
         return carry
 
     lax.fori_loop(0, 2 * chips, block, 0)
@@ -322,7 +307,7 @@
             coords,
             coords,
             jnp.zeros((chans, HALF - dirs - 9, per_dev), jnp.float32),
-            size,
+            2.0 * size,
             jnp.zeros((chans, GROUP - HALF - dirs, per_dev), jnp.float32),
         ],
         1,
@@ -354,6 +339,7 @@
             pltpu.VMEM((devices,) + own_sources.shape, jnp.float32),
             pltpu.VMEM((2 * wide, 4 * GROUP), jnp.bfloat16),
             pltpu.VMEM((4 * GROUP, width), jnp.bfloat16),
+            pltpu.VMEM((2, wide, width), jnp.bfloat16),
             pltpu.VMEM((wide, wide), jnp.float32),
         ]
         + [pltpu.SemaphoreType.DMA((chips,))] * 8

time: 61.3 us -> 43.2 us (0.70)
  Pallas kernels: 55 us -> 36.8 us
    pallas_call x1, Pallas kernels: 55 us -> 36.8 us  [on_device(): pl.pallas_call(functools.partial(kernel, devices, chans, dirs, scale), ou...]
where the time goes in v2:
time: 43.2 us; the launch traced here: 42.8 us
  Pallas kernels  36.8 us (85%)
  local copies, waits for them, and re-layouts  4.19 us (10%)
  other arithmetic  1.69 us (4%)
    pallas_call x1, Pallas kernels, on_device(): pl.pallas_call(functools.partial(kernel, devices, chans, dirs, scale), ou...  36.8 us
    unnamed x16, local copies, waits for them, and re-layouts  3.29 us

profile of v2, /device:TPU:31, one launch (start us, length us, event | category | flops | bytes accessed | tf_op | source)
XLA Modules:
  0.0 42.8 jit_solution(7512642406967076349)
XLA Ops:
  0.0 0.0 copy-start
  0.0 0.9 %fusion.5 = f32[4,16,32]{2,1,0:T(8,128)S(1)} fusion(f32[4,2,16,32]{3,2,1,0:T(8,128)} %param.10), kind=kLoop, calls=%fused_computation.6 | loop fusion | flops 22528 | bytes 24576 | tf_op jit(solution)/shard_map/mul | solution.py:310
  0.9 0.0 copy-done
  0.9 0.0 copy-start.6
  0.9 0.0 copy-start.4
  0.9 0.1 fusion.7
  1.0 0.6 %copy-done.6 = s32[4]{0:T(128)S(1)} copy-done((s32[4]{0:T(128)S(1)}, s32[4]{0:T(128)}, u32[]{:S(2)}) %copy-start.6) | copy-done | bytes 40
  1.5 0.0 copy-done.4
  1.6 0.1 broadcast_multiply_fusion
  1.7 0.1 concatenate.6
  1.8 0.0 copy-start.3
  1.8 0.0 copy-start.1
  1.8 0.7 %copy.12 = f32[2,128,32]{1,2,0:T(8,128)} copy(f32[2,128,32]{2,1,0:T(8,128)S(1)} %bitcast.31) | data formatting | bytes 65536 | tf_op jit(solution)/shard_map/reshape | solution.py:316
  2.5 0.0 copy-start.2
  2.5 0.0 copy-done.3
  2.5 0.1 pad.3.clone
  2.6 0.0 copy-done.1
  2.6 0.6 %copy-done.2 = f32[2,1024]{1,0:T(2,128)S(1)} copy-done((f32[2,1024]{1,0:T(2,128)S(1)}, f32[2,1024]{1,0:T(2,128)}, u32[]{:S(2)}) %copy-start.2) | copy-done | bytes 8216
  3.2 0.0 copy-start.5
  3.2 0.7 %maximum_maximum_fusion.source_ref = f32[8,1024]{1,0:T(8,128)} fusion(f32[1,1024]{1,0:T(1,128)S(1)} %bitcast.33, f32[4,1024]{1,0:T(4,128)S(1)} %copy-done.1, f32[2,1024]{1,0:T(2,128)S(1)} %copy-done.2, f32[8]{0:T(128)S(1)} %pad.3.clone), kind=kLoop, calls=%fused_computation.7 | loop fusion | flops 24576 | bytes 61472 | tf_op jit(solution)/shard_map/concatenate | solution.py:320
  3.9 0.0 copy-done.5
  3.9 0.7 %copy.13.tile_ref = s32[16,2]{1,0:T(8,128)} copy(s32[16,2]{0,1:T(2,128)S(1)} %copy-done.5) | data formatting | bytes 256 | tf_op args[6]
  4.6 36.8 %shard_map.73 = f32[1,4,2,1024]{3,2,1,0:T(2,128)} custom-call(s32[16,2]{1,0:T(8,128)} %copy.13.tile_ref, f32[64,128]{1,0:T(8,128)} %bitcast.32, f32[8,1024]{1,0:T(8,128)} %maximum_maximum_fusion.source_ref), custom_call_target="tpu_custom_call" | custom-call | tf_op jit(solution)/shard_map/pallas_call | solution.py:332
  41.4 1.4 %copy.16 = f32[1,4,2,1024]{3,2,1,0:T(2,128)} copy(f32[1,4,2,1024]{3,2,1,0:T(2,128)} %shard_map.73) | data formatting | bytes 65536
  (4 shorter events, 0.0 us)
Async XLA Ops:
  0.0 0.9 %copy-start = (f32[4,2,16,32]{3,2,1,0:T(8,128)S(1)}, f32[4,2,16,32]{3,2,1,0:T(8,128)}, u32[]{:S(2)}) copy-start(f32[4,2,16,32]{3,2,1,0:T(8,128)} %param.10) | copy-start | bytes 49156
  0.9 0.7 %copy-start.6 = (s32[4]{0:T(128)S(1)}, s32[4]{0:T(128)}, u32[]{:S(2)}) copy-start(s32[4]{0:T(128)} %param.12) | copy-start | bytes 52
  0.9 0.7 %copy-start.4 = (f32[3,32]{1,0:T(4,128)S(1)}, f32[3,32]{1,0:T(4,128)}, u32[]{:S(2)}) copy-start(f32[3,32]{1,0:T(4,128)} %param.11) | copy-start | bytes 1156
  1.8 0.7 %copy-start.3 = (s32[1024]{0:T(1024)S(1)}, s32[1024]{0:T(1024)}, u32[]{:S(2)}) copy-start(s32[1024]{0:T(1024)} %param.9) | copy-start | bytes 12292
  1.8 0.8 %copy-start.1 = (f32[4,1024]{1,0:T(4,128)S(1)}, f32[4,1024]{1,0:T(4,128)}, u32[]{:S(2)}) copy-start(f32[4,1024]{1,0:T(4,128)} %param.8) | copy-start | bytes 49156
  2.5 0.7 %copy-start.2 = (f32[2,1024]{1,0:T(2,128)S(1)}, f32[2,1024]{1,0:T(2,128)}, u32[]{:S(2)}) copy-start(f32[2,1024]{1,0:T(2,128)} %param.7) | copy-start | bytes 24580
  3.2 0.7 %copy-start.5 = (s32[16,2]{0,1:T(2,128)S(1)}, s32[16,2]{0,1:T(2,128)}, u32[]{:S(2)}) copy-start(s32[16,2]{0,1:T(2,128)} %param.13) | copy-start | bytes 388

commit v3 on v2

--- a/solution.py
+++ b/solution.py
@@ -11,9 +11,20 @@
 MESH = pl.DeviceIdType.MESH
 TS = 32
 GROUP = 64
-HALF = 32
+HALF = 48
 CHUNK = 256
 SINE = (3.1415820121765137, -5.167142868041992, 2.5418992042541504, -0.5546366572380066)
+ATAN = (
+    0.15915492177009583,
+    -0.05305047705769539,
+    0.031808558851480484,
+    -0.022538291290402412,
+    0.016709571704268456,
+    -0.011514591053128242,
+    0.006331328768283129,
+    -0.0022920165210962296,
+    0.00039099203422665596,
+)
 ONE = 1.0 + 6e-7
 
 
@@ -29,6 +40,18 @@
     rest = value - first
     second = rest.astype(jnp.bfloat16).astype(jnp.float32)
     return first, second, rest - second
+
+
+def polar(real, imag):
+    wide, tall = jnp.abs(real), jnp.abs(imag)
+    large, small = jnp.maximum(wide, tall), jnp.minimum(wide, tall)
+    ratio = small / jnp.where(large > 0.0, large, 1.0)
+    square = ratio * ratio
+    size = large * jnp.sqrt(1.0 + square)
+    angle = ratio * horner(ATAN, square)
+    angle = jnp.where(tall > wide, 0.25 - angle, angle)
+    angle = jnp.where(real < 0.0, 0.5 - angle, angle)
+    return size, jnp.where(imag < 0.0, -angle, angle)
 
 
 def kernel(
@@ -37,8 +60,12 @@
     dirs,
     scale,
     tile_ref,
-    station_ref,
-    source_ref,
+    channel_ref,
+    position_ref,
+    flux_ref,
+    cluster_ref,
+    jones_ref,
+    uvw_ref,
     out_ref,
     stations,
     sources,
@@ -54,7 +81,6 @@
     so_recv,
     so_fwd_send,
     so_fwd_recv,
-    own_sem,
 ):
     chips = devices // 2
     me = lax.axis_index("src")
@@ -65,13 +91,6 @@
     per_dev = rows * 2 // chans
     width = sources.shape[2]
 
-    own = [
-        pltpu.make_async_copy(station_ref, stations.at[me], own_sem.at[0]),
-        pltpu.make_async_copy(source_ref, sources.at[me], own_sem.at[1]),
-    ]
-    for copy in own:
-        copy.start()
-
     barrier = pltpu.get_barrier_semaphore()
 
     def greet(k, carry):
@@ -81,6 +100,26 @@
 
     pl.semaphore_signal(barrier, inc=1, device_id={"src": partner}, device_id_type=MESH)
     lax.fori_loop(1, chips, greet, 0)
+
+    l_own, m_own = position_ref[0:1, :], position_ref[1:2, :]
+    sources[me, 0:2, :] = position_ref[...]
+    sources[me, 2 : 2 + chans, :] = flux_ref[...]
+    sources[me, 2 + chans : 3 + chans, :] = cluster_ref[...].astype(jnp.float32)
+    sources[me, 3 + chans : 4 + chans, :] = jnp.sqrt(1.0 - l_own * l_own - m_own * m_own) - 1.0
+    eight = lax.broadcasted_iota(jnp.int32, (8, per_dev), 0)
+    coords = jnp.where(eight == 0, uvw_ref[0:1, :], 0.0)
+    coords = jnp.where(eight == 1, uvw_ref[1:2, :], coords)
+    coords = jnp.where(eight == 3 + chans, uvw_ref[2:3, :], coords)
+    for pair in range(chans // 2):
+        features = []
+        for c in (2 * pair, 2 * pair + 1):
+            freq_ratio = 1.0 + 0.002 * channel_ref[c].astype(jnp.float32)
+            size, angle = polar(jones_ref[c, 0], jones_ref[c, 1])
+            shifted = coords * freq_ratio
+            features += [-angle, shifted, shifted, shifted]
+            features += [jnp.zeros((HALF - dirs - 24, per_dev), jnp.float32), 2.0 * size]
+        stations[me, pair * per_dev : (pair + 1) * per_dev, :] = jnp.concatenate(features, 0).T
+
     pl.semaphore_wait(barrier, chips)
 
     def direct(mine, slots, send, recv, k):
@@ -127,36 +166,30 @@
             device_id_type=MESH,
         )
 
-    for copy in own:
-        copy.wait()
     forward(stations, st_fwd_send, st_fwd_recv, 0).start()
 
     def send_stations(k, carry):
-        direct(station_ref, stations, st_send, st_recv, k).start()
+        direct(stations.at[me], stations, st_send, st_recv, k).start()
         return carry
 
     lax.fori_loop(1, chips, send_stations, 0)
+    onehots[3 * GROUP :, :] = jnp.zeros((GROUP, width), jnp.bfloat16)
+    acc[...] = jnp.zeros_like(acc)
+
+    def relay_stations(k, carry):
+        arrival(stations.at[me], stations, st_send, st_recv, k).wait_recv()
+        forward(stations, st_fwd_send, st_fwd_recv, k).start()
+        return carry
+
+    lax.fori_loop(1, chips, relay_stations, 0)
+
     forward(sources, so_fwd_send, so_fwd_recv, 0).start()
 
     def send_sources(k, carry):
-        direct(source_ref, sources, so_send, so_recv, k).start()
+        direct(sources.at[me], sources, so_send, so_recv, k).start()
         return carry
 
     lax.fori_loop(1, chips, send_sources, 0)
-
-    onehots[3 * GROUP :, :] = jnp.zeros((GROUP, width), jnp.bfloat16)
-    for part in range(3):
-        onehots[part * GROUP + HALF + dirs : (part + 1) * GROUP, :] = jnp.zeros(
-            (GROUP - HALF - dirs, width), jnp.bfloat16
-        )
-    acc[...] = jnp.zeros_like(acc)
-
-    def relay_stations(k, carry):
-        arrival(station_ref, stations, st_send, st_recv, k).wait_recv()
-        forward(stations, st_fwd_send, st_fwd_recv, k).start()
-        return carry
-
-    lax.fori_loop(1, chips, relay_stations, 0)
 
     def take_stations(k, carry):
         forwarded(stations, st_fwd_send, st_fwd_recv, k).wait_recv()
@@ -195,7 +228,7 @@
 
         @pl.when(jnp.logical_and(odd == 0, k > 0))
         def _():
-            arrival(source_ref, sources, so_send, so_recv, k).wait_recv()
+            arrival(sources.at[me], sources, so_send, so_recv, k).wait_recv()
             forward(sources, so_fwd_send, so_fwd_recv, k).start()
 
         @pl.when(odd == 1)
@@ -204,23 +237,17 @@
 
         flip = core + odd - 2 * core * odd
         came = lax.rem(chip - k + chips, chips) * 2 + flip
-        l_term = sources[came, 0:1, :]
-        m_term = sources[came, 1:2, :]
-        kinds = sources[came, 2 + chans : 3 + chans, :]
-        n_less = jnp.sqrt(1.0 - l_term * l_term - m_term * m_term) - 1.0
-        sub = lax.broadcasted_iota(jnp.int32, (16, width), 0)
-        coords = jnp.zeros((16, width), jnp.float32)
-        for axis, term in enumerate((l_term, m_term, n_less)):
-            for index, part in enumerate(three_parts(term)):
-                coords = jnp.where(sub == index * 3 + axis, part, coords)
+        rows_in = sources[came]
+        kinds = rows_in[2 + chans : 3 + chans, :]
+        parts = three_parts(rows_in) + (jnp.zeros_like(rows_in),)
         kind_rows = lax.broadcasted_iota(jnp.int32, (dirs, width), 0).astype(jnp.float32)
         onehot = jnp.where(kind_rows == kinds, 1.0, 0.0).astype(jnp.bfloat16)
-        coords = coords.astype(jnp.bfloat16)
+        upper = jnp.concatenate(parts[:2], 0).astype(jnp.bfloat16)
+        lower = jnp.concatenate(parts[2:], 0).astype(jnp.bfloat16)
         for part in range(3):
             base = part * GROUP
-            onehots[base : base + dirs, :] = onehot
-            onehots[base + dirs : base + dirs + 16, :] = coords
-            onehots[base + HALF : base + HALF + dirs, :] = onehot
+            for index, value in enumerate((onehot, upper, lower, onehot)):
+                onehots[base + index * 16 : base + index * 16 + 16, :] = value
 
         for chunk in range(width // CHUNK):
             cols = slice(chunk * CHUNK, chunk * CHUNK + CHUNK)
@@ -273,8 +300,8 @@
                 out_ref[0, c, part : part + 1, i * TS : i * TS + TS] = value[i : i + 1, :]
 
     def finish(k, carry):
-        direct(station_ref, stations, st_send, st_recv, k).wait_send()
-        direct(source_ref, sources, so_send, so_recv, k).wait_send()
+        direct(stations.at[me], stations, st_send, st_recv, k).wait_send()
+        direct(sources.at[me], sources, so_send, so_recv, k).wait_send()
         return carry
 
     lax.fori_loop(1, chips, finish, 0)
@@ -288,64 +315,30 @@
 
 
 def on_device(positions, flux, cluster, jones, station_uvw, channels, tile_map):
-    freq_ratio = 1.0 + 0.002 * channels.astype(jnp.float32)
     width = positions.shape[1]
     devices = lax.axis_size("src")
     scale = 1.0 / math.sqrt(width * devices)
     chans, _, dirs, per_dev = jones.shape
 
-    large = jnp.maximum(jnp.abs(jones[:, 0]), jnp.abs(jones[:, 1]))
-    small = jnp.minimum(jnp.abs(jones[:, 0]), jnp.abs(jones[:, 1]))
-    ratio = small / jnp.where(large > 0.0, large, 1.0)
-    size = large * jnp.sqrt(1.0 + ratio * ratio)
-    angle = jnp.arctan2(jones[:, 1], jones[:, 0]) * (-0.5 / math.pi)
-    coords = freq_ratio[:, None, None] * station_uvw[None]
-    features = jnp.concatenate(
-        [
-            angle,
-            coords,
-            coords,
-            coords,
-            jnp.zeros((chans, HALF - dirs - 9, per_dev), jnp.float32),
-            2.0 * size,
-            jnp.zeros((chans, GROUP - HALF - dirs, per_dev), jnp.float32),
-        ],
-        1,
-    )
-    own_stations = (
-        features.reshape(chans // 2, 2 * GROUP, per_dev)
-        .transpose(0, 2, 1)
-        .reshape(chans // 2 * per_dev, 2 * GROUP)
-    )
-    own_sources = jnp.concatenate(
-        [
-            positions,
-            flux,
-            cluster.astype(jnp.float32)[None],
-            jnp.zeros((8 - 3 - chans, width), jnp.float32),
-        ],
-        0,
-    )
     wide = 2 * chans * TS
     chips = devices // 2
     vmem = pl.BlockSpec(memory_space=pltpu.VMEM)
     return pl.pallas_call(
         functools.partial(kernel, devices, chans, dirs, scale),
         out_shape=jax.ShapeDtypeStruct((1, chans, 2, TS * TS), jnp.float32),
-        in_specs=[pl.BlockSpec(memory_space=pltpu.SMEM), vmem, vmem],
+        in_specs=[pl.BlockSpec(memory_space=pltpu.SMEM)] * 2 + [vmem] * 5,
         out_specs=vmem,
         scratch_shapes=[
-            pltpu.VMEM((devices,) + own_stations.shape, jnp.float32),
-            pltpu.VMEM((devices,) + own_sources.shape, jnp.float32),
+            pltpu.VMEM((devices, chans // 2 * per_dev, 2 * GROUP), jnp.float32),
+            pltpu.VMEM((devices, 8, width), jnp.float32),
             pltpu.VMEM((2 * wide, 4 * GROUP), jnp.bfloat16),
             pltpu.VMEM((4 * GROUP, width), jnp.bfloat16),
             pltpu.VMEM((2, wide, width), jnp.bfloat16),
             pltpu.VMEM((wide, wide), jnp.float32),
         ]
-        + [pltpu.SemaphoreType.DMA((chips,))] * 8
-        + [pltpu.SemaphoreType.DMA((2,))],
+        + [pltpu.SemaphoreType.DMA((chips,))] * 8,
         compiler_params=pltpu.CompilerParams(collective_id=0, has_side_effects=True),
-    )(tile_map, own_stations, own_sources)
+    )(tile_map, channels, positions, flux, cluster[None], jones, station_uvw)
 
 
 def solution(mesh):

time: 43.2 us -> 39.4 us (0.912)
  the two profiles are of different devices: /device:TPU:31 before, /device:TPU:0 now
where the time goes in v3:
time: 39.4 us; the launch traced here: 39.1 us
  Pallas kernels  36.4 us (92%)
  local copies, waits for them, and re-layouts  2.73 us (7%)
    pallas_call x1, Pallas kernels, on_device(): pl.pallas_call(functools.partial(kernel, devices, chans, dirs, scale), ou...  36.4 us
    unnamed x4, local copies, waits for them, and re-layouts  2.73 us

profile of v3, /device:TPU:0, one launch (start us, length us, event | category | flops | bytes accessed | tf_op | source)
XLA Modules:
  0.0 39.1 jit_solution(16086819245034161880)
XLA Ops:
  0.0 0.0 copy-start
  0.0 0.7 %copy-done = s32[16,2]{0,1:T(2,128)S(1)} copy-done((s32[16,2]{0,1:T(2,128)S(1)}, s32[16,2]{0,1:T(2,128)}, u32[]{:S(2)}) %copy-start) | copy-done | bytes 152
  0.7 0.7 %copy.8.tile_ref = s32[16,2]{1,0:T(8,128)} copy(s32[16,2]{0,1:T(2,128)S(1)} %copy-done) | data formatting | bytes 256 | tf_op args[6]
  1.4 36.4 %shard_map.73 = f32[1,4,2,1024]{3,2,1,0:T(2,128)} custom-call(s32[16,2]{1,0:T(8,128)} %copy.8.tile_ref, s32[4]{0:T(128)} %channel_ref.1, f32[2,1024]{1,0:T(2,128)} %position_ref.1, f32[4,1024]{1,0:T(4,128)} %flux_ref.1, s32[1,1024]{1,0:T(1,128)} %bitcast.1, f32[4,2,16,32]{3,2,1,0:T(8,128)} %jones_ref.1, f32[3,32]{1,0:T(4,128)} %uvw_ref.1), custom_call_target="tpu_custom_call" | custom-call | tf_op jit(solution)/shard_map/pallas_call | solution.py:326
  37.8 1.4 %copy.10 = f32[1,4,2,1024]{3,2,1,0:T(2,128)} copy(f32[1,4,2,1024]{3,2,1,0:T(2,128)} %shard_map.73) | data formatting | bytes 65536
Async XLA Ops:
  0.0 0.7 %copy-start = (s32[16,2]{0,1:T(2,128)S(1)}, s32[16,2]{0,1:T(2,128)}, u32[]{:S(2)}) copy-start(s32[16,2]{0,1:T(2,128)} %param.13) | copy-start | bytes 388

commit v4 on v3

--- a/solution.py
+++ b/solution.py
@@ -173,7 +173,8 @@
         return carry
 
     lax.fori_loop(1, chips, send_stations, 0)
-    onehots[3 * GROUP :, :] = jnp.zeros((GROUP, width), jnp.bfloat16)
+    onehots[:, 3 * GROUP :, :] = jnp.zeros((2, GROUP, width), jnp.bfloat16)
+    sides[1] = jnp.zeros(sides.shape[1:], jnp.bfloat16)
     acc[...] = jnp.zeros_like(acc)
 
     def relay_stations(k, carry):
@@ -222,21 +223,9 @@
                     jnp.bfloat16
                 )
 
-    def block(step, carry):
-        k = step // 2
-        odd = lax.rem(step, 2)
-
-        @pl.when(jnp.logical_and(odd == 0, k > 0))
-        def _():
-            arrival(sources.at[me], sources, so_send, so_recv, k).wait_recv()
-            forward(sources, so_fwd_send, so_fwd_recv, k).start()
-
-        @pl.when(odd == 1)
-        def _():
-            forwarded(sources, so_fwd_send, so_fwd_recv, k).wait_recv()
-
-        flip = core + odd - 2 * core * odd
-        came = lax.rem(chip - k + chips, chips) * 2 + flip
+    contract = (((1,), (1,)), ((), ()))
+
+    def predict(slot, came):
         rows_in = sources[came]
         kinds = rows_in[2 + chans : 3 + chans, :]
         parts = three_parts(rows_in) + (jnp.zeros_like(rows_in),)
@@ -247,11 +236,11 @@
         for part in range(3):
             base = part * GROUP
             for index, value in enumerate((onehot, upper, lower, onehot)):
-                onehots[base + index * 16 : base + index * 16 + 16, :] = value
+                onehots[slot, base + index * 16 : base + index * 16 + 16, :] = value
 
         for chunk in range(width // CHUNK):
             cols = slice(chunk * CHUNK, chunk * CHUNK + CHUNK)
-            weights = onehots[:, cols]
+            weights = onehots[slot, :, cols]
             found = jnp.dot(table[...], weights, preferred_element_type=jnp.float32)
             for side in range(2):
                 for c in range(chans):
@@ -268,19 +257,32 @@
                     real = double * (0.5 - square)
                     imag = (double * sine) * cosine
                     top = c * TS
-                    sides[side, top : top + TS, cols] = real.astype(jnp.bfloat16)
-                    sides[side, half_rows + top : half_rows + top + TS, cols] = imag.astype(
+                    sides[slot, side, top : top + TS, cols] = real.astype(jnp.bfloat16)
+                    sides[slot, side, half_rows + top : half_rows + top + TS, cols] = imag.astype(
                         jnp.bfloat16
                     )
+
+    def add_products(slot):
         acc[...] += lax.dot_general(
-            sides[0],
-            sides[1],
-            (((1,), (1,)), ((), ())),
-            preferred_element_type=jnp.float32,
-        )
-        return carry
-
-    lax.fori_loop(0, 2 * chips, block, 0)
+            sides[slot, 0], sides[slot, 1], contract, preferred_element_type=jnp.float32
+        )
+
+    def step(k, carry):
+        @pl.when(k > 0)
+        def _():
+            arrival(sources.at[me], sources, so_send, so_recv, k).wait_recv()
+            forward(sources, so_fwd_send, so_fwd_recv, k).start()
+
+        forwarded(sources, so_fwd_send, so_fwd_recv, k).wait_recv()
+        came = lax.rem(chip - k + chips, chips) * 2
+        predict(0, came + core)
+        add_products(1)
+        predict(1, came + 1 - core)
+        add_products(0)
+        return carry
+
+    lax.fori_loop(0, chips, step, 0)
+    add_products(1)
 
     same = tiles[0] == tiles[1]
     diagonal = lax.broadcasted_iota(jnp.int32, (TS, TS), 0) == lax.broadcasted_iota(
@@ -332,8 +334,8 @@
             pltpu.VMEM((devices, chans // 2 * per_dev, 2 * GROUP), jnp.float32),
             pltpu.VMEM((devices, 8, width), jnp.float32),
             pltpu.VMEM((2 * wide, 4 * GROUP), jnp.bfloat16),
-            pltpu.VMEM((4 * GROUP, width), jnp.bfloat16),
-            pltpu.VMEM((2, wide, width), jnp.bfloat16),
+            pltpu.VMEM((2, 4 * GROUP, width), jnp.bfloat16),
+            pltpu.VMEM((2, 2, wide, width), jnp.bfloat16),
             pltpu.VMEM((wide, wide), jnp.float32),
         ]
         + [pltpu.SemaphoreType.DMA((chips,))] * 8,

time: 39.4 us -> 42.3 us (1.074)
  the two profiles are of different devices: /device:TPU:0 before, /device:TPU:1 now
where the time goes in v4:
time: 42.3 us; the launch traced here: 42 us
  Pallas kernels  39.3 us (93%)
  local copies, waits for them, and re-layouts  2.73 us (6%)
    pallas_call x1, Pallas kernels, on_device(): pl.pallas_call(functools.partial(kernel, devices, chans, dirs, scale), ou...  39.3 us
    unnamed x4, local copies, waits for them, and re-layouts  2.73 us

profile of v4, /device:TPU:1, one launch (start us, length us, event | category | flops | bytes accessed | tf_op | source)
XLA Modules:
  0.0 42.0 jit_solution(16887095299661796673)
XLA Ops:
  0.0 0.0 copy-start
  0.0 0.7 %copy-done = s32[16,2]{0,1:T(2,128)S(1)} copy-done((s32[16,2]{0,1:T(2,128)S(1)}, s32[16,2]{0,1:T(2,128)}, u32[]{:S(2)}) %copy-start) | copy-done | bytes 152
  0.7 0.7 %copy.8.tile_ref = s32[16,2]{1,0:T(8,128)} copy(s32[16,2]{0,1:T(2,128)S(1)} %copy-done) | data formatting | bytes 256 | tf_op args[6]
  1.4 39.3 %shard_map.73 = f32[1,4,2,1024]{3,2,1,0:T(2,128)} custom-call(s32[16,2]{1,0:T(8,128)} %copy.8.tile_ref, s32[4]{0:T(128)} %channel_ref.1, f32[2,1024]{1,0:T(2,128)} %position_ref.1, f32[4,1024]{1,0:T(4,128)} %flux_ref.1, s32[1,1024]{1,0:T(1,128)} %bitcast.1, f32[4,2,16,32]{3,2,1,0:T(8,128)} %jones_ref.1, f32[3,32]{1,0:T(4,128)} %uvw_ref.1), custom_call_target="tpu_custom_call" | custom-call | tf_op jit(solution)/shard_map/pallas_call | solution.py:328
  40.6 1.4 %copy.10 = f32[1,4,2,1024]{3,2,1,0:T(2,128)} copy(f32[1,4,2,1024]{3,2,1,0:T(2,128)} %shard_map.73) | data formatting | bytes 65536
Async XLA Ops:
  0.0 0.7 %copy-start = (s32[16,2]{0,1:T(2,128)S(1)}, s32[16,2]{0,1:T(2,128)}, u32[]{:S(2)}) copy-start(s32[16,2]{0,1:T(2,128)} %param.13) | copy-start | bytes 388

commit v5 on v4

--- a/solution.py
+++ b/solution.py
@@ -173,6 +173,14 @@
         return carry
 
     lax.fori_loop(1, chips, send_stations, 0)
+    forward(sources, so_fwd_send, so_fwd_recv, 0).start()
+
+    def send_sources(k, carry):
+        direct(sources.at[me], sources, so_send, so_recv, k).start()
+        return carry
+
+    lax.fori_loop(1, chips, send_sources, 0)
+
     onehots[:, 3 * GROUP :, :] = jnp.zeros((2, GROUP, width), jnp.bfloat16)
     sides[1] = jnp.zeros(sides.shape[1:], jnp.bfloat16)
     acc[...] = jnp.zeros_like(acc)
@@ -183,14 +191,6 @@
         return carry
 
     lax.fori_loop(1, chips, relay_stations, 0)
-
-    forward(sources, so_fwd_send, so_fwd_recv, 0).start()
-
-    def send_sources(k, carry):
-        direct(sources.at[me], sources, so_send, so_recv, k).start()
-        return carry
-
-    lax.fori_loop(1, chips, send_sources, 0)
 
     def take_stations(k, carry):
         forwarded(stations, st_fwd_send, st_fwd_recv, k).wait_recv()
@@ -268,15 +268,16 @@
         )
 
     def step(k, carry):
-        @pl.when(k > 0)
-        def _():
-            arrival(sources.at[me], sources, so_send, so_recv, k).wait_recv()
-            forward(sources, so_fwd_send, so_fwd_recv, k).start()
-
-        forwarded(sources, so_fwd_send, so_fwd_recv, k).wait_recv()
         came = lax.rem(chip - k + chips, chips) * 2
         predict(0, came + core)
         add_products(1)
+
+        @pl.when(k + 1 < chips)
+        def _():
+            arrival(sources.at[me], sources, so_send, so_recv, k + 1).wait_recv()
+            forward(sources, so_fwd_send, so_fwd_recv, k + 1).start()
+
+        forwarded(sources, so_fwd_send, so_fwd_recv, k).wait_recv()
         predict(1, came + 1 - core)
         add_products(0)
         return carry

time: 42.3 us -> 36.2 us (0.86)
  the two profiles are of different devices: /device:TPU:1 before, /device:TPU:31 now
where the time goes in v5:
time: 36.2 us; the launch traced here: 35.9 us
  Pallas kernels  33.2 us (92%)
  local copies, waits for them, and re-layouts  2.73 us (8%)
    pallas_call x1, Pallas kernels, on_device(): pl.pallas_call(functools.partial(kernel, devices, chans, dirs, scale), ou...  33.2 us
    unnamed x4, local copies, waits for them, and re-layouts  2.73 us

profile of v5, /device:TPU:31, one launch (start us, length us, event | category | flops | bytes accessed | tf_op | source)
XLA Modules:
  0.0 35.9 jit_solution(2702561741440790872)
XLA Ops:
  0.0 0.0 copy-start
  0.0 0.7 %copy-done = s32[16,2]{0,1:T(2,128)S(1)} copy-done((s32[16,2]{0,1:T(2,128)S(1)}, s32[16,2]{0,1:T(2,128)}, u32[]{:S(2)}) %copy-start) | copy-done | bytes 152
  0.7 0.7 %copy.8.tile_ref = s32[16,2]{1,0:T(8,128)} copy(s32[16,2]{0,1:T(2,128)S(1)} %copy-done) | data formatting | bytes 256 | tf_op args[6]
  1.4 33.2 %shard_map.73 = f32[1,4,2,1024]{3,2,1,0:T(2,128)} custom-call(s32[16,2]{1,0:T(8,128)} %copy.8.tile_ref, s32[4]{0:T(128)} %channel_ref.1, f32[2,1024]{1,0:T(2,128)} %position_ref.1, f32[4,1024]{1,0:T(4,128)} %flux_ref.1, s32[1,1024]{1,0:T(1,128)} %bitcast.1, f32[4,2,16,32]{3,2,1,0:T(8,128)} %jones_ref.1, f32[3,32]{1,0:T(4,128)} %uvw_ref.1), custom_call_target="tpu_custom_call" | custom-call | tf_op jit(solution)/shard_map/pallas_call | solution.py:329
  34.5 1.4 %copy.10 = f32[1,4,2,1024]{3,2,1,0:T(2,128)} copy(f32[1,4,2,1024]{3,2,1,0:T(2,128)} %shard_map.73) | data formatting | bytes 65536
Async XLA Ops:
  0.0 0.7 %copy-start = (s32[16,2]{0,1:T(2,128)S(1)}, s32[16,2]{0,1:T(2,128)}, u32[]{:S(2)}) copy-start(s32[16,2]{0,1:T(2,128)} %param.13) | copy-start | bytes 388
